TPU v7x, 32 devices: a whole 2x2x4 slice. The times are simulated.
32 devices in a mesh: groups: 2 (over y), blk: 4 (over z), rep: 4 (over x, core).
Axes of the slice: x: 2, y: 2, z: 4, core: 2. Of those that a mesh axis runs over, the one named last changes fastest.
Arguments:
- embeddings: float32 [8192, 128], P(('groups', 'blk')), parts along dimension 0, may hold values from -6 to 6
- degrees: int32 [8192], P(('groups', 'blk')), parts along dimension 0, may hold values from 1 to 12800, as said below
- tile_values: bfloat16 [8, 4, 1, 24, 128, 128], P(('groups', 'blk'), 'rep'), parts along dimension 0
- tile_rows: int32 [8, 4, 1, 24], P(('groups', 'blk'), 'rep'), parts along dimension 0, may hold values from 0 to 7
- tile_columns: int32 [8, 4, 1, 24], P(('groups', 'blk'), 'rep'), parts along dimension 0, may hold values from 0 to 7
- slot_counts: int32 [8, 4, 1], P(('groups', 'blk'), 'rep'), parts along dimension 0, may hold values from 6 to 24, as said below
Outputs:
- combined: float32 [8192, 128], P(('groups', 'blk', 'rep')), parts along dimension 0
There are 2 independent parts, one for each index of `groups`. A program takes and returns all parts, laid end to end along the dimension named above; each array names one. Nothing has to cross between parts.
Inputs may be any that keep to these rules, and one draw needn't show every extreme that they name: `degrees`: each node's degree is at least the number of nonzero entries in its row of A. `slot_counts`: some arc position of some device has all 24 slots live in every draw.
All inputs are finite; a program needn't handle non-finite values.
Results may differ from a plain program's by a relative error of at most 0.0003.
Values sent between devices are 32-bit elements; how exact they have to be, the bound alone decides.
A program may use at most 64 MiB of HBM per device.

v0:
```python
import jax
import jax.numpy as jnp
from jax import lax
from jax.sharding import PartitionSpec as P

LAYERS = 2


def shifted_2(shard, axis, by):
    devices = lax.axis_size(axis)
    return lax.ppermute(shard, axis, [(i, (i + by) % devices) for i in range(devices)])


def slot_term(source_panel, arc_slot, slots):
    tile_values, tile_rows, tile_columns, slot_counts = slots
    slot_total = tile_values.shape[1]
    block_total = source_panel.shape[0]
    columns = lax.dynamic_index_in_dim(tile_columns, arc_slot, 0, keepdims=False)
    values = lax.dynamic_index_in_dim(tile_values, arc_slot, 0, keepdims=False)
    row_blocks = lax.dynamic_index_in_dim(tile_rows, arc_slot, 0, keepdims=False)
    live_count = lax.dynamic_index_in_dim(slot_counts, arc_slot, 0, keepdims=False)
    blocks = jnp.take(source_panel, columns, axis=0)
    products = jnp.einsum(
        "jab,jbw->jaw",
        values,
        blocks,
        precision=lax.Precision.HIGHEST,
        preferred_element_type=jnp.float32,
    )
    live_slots = jnp.arange(slot_total, dtype=jnp.int32) < live_count
    placement = (
        (row_blocks[:, None] == jnp.arange(block_total, dtype=jnp.int32)[None, :])
        & live_slots[:, None]
    ).astype(jnp.float32)
    return jnp.einsum("jc,jaw->caw", placement, products, precision=lax.Precision.HIGHEST)


def arc_product(source_panel, slots, team_index, team_count):
    arc_length = slots[0].shape[0]
    arc_panel = source_panel
    for power_index in range(team_count.bit_length() - 1):
        shifted = shifted_2(arc_panel, "blk", arc_length * (1 << power_index))
        arc_panel = jnp.where(team_index >> power_index & 1 == 1, shifted, arc_panel)
    empty = jnp.zeros(source_panel.shape, jnp.float32)

    def walk(arc_slot, loop_state):
        partial_value, panel_now = loop_state
        partial_value = partial_value + slot_term(panel_now, arc_slot, slots)
        panel_now = shifted_2(panel_now, "blk", 1)
        return (partial_value, panel_now)

    partial_value, panel_now = lax.fori_loop(0, arc_length - 1, walk, (empty, arc_panel))
    return partial_value + slot_term(panel_now, arc_length - 1, slots)


def per_device(embeddings, degrees, tile_values, tile_rows, tile_columns, slot_counts):
    tile_size = tile_values.shape[-1]
    width_count = embeddings.shape[1]
    block_count = embeddings.shape[0] // tile_size
    slots = (tile_values[0, 0], tile_rows[0, 0], tile_columns[0, 0], slot_counts[0, 0])
    team_index = lax.axis_index("rep")
    team_count = lax.axis_size("rep")
    share_rows = embeddings.shape[0] // team_count
    norm_scale = lax.rsqrt(degrees.astype(jnp.float32))
    current = embeddings
    combined = lax.dynamic_slice_in_dim(embeddings, team_index * share_rows, share_rows)
    for layer_index in range(LAYERS):
        source_panel = (current * norm_scale[:, None]).reshape(block_count, tile_size, width_count)
        partial_value = arc_product(source_panel, slots, team_index, team_count)
        partial_value = partial_value.reshape(block_count * tile_size, width_count)
        current = lax.psum(partial_value, "rep") * norm_scale[:, None]
        combined = combined + lax.dynamic_slice_in_dim(current, team_index * share_rows, share_rows)
    return combined / (LAYERS + 1.0)


def solution(mesh):
    in_specs = (
        P(("groups", "blk"), None),
        P(("groups", "blk")),
        P(("groups", "blk"), "rep", None, None, None, None),
        P(("groups", "blk"), "rep", None, None),
        P(("groups", "blk"), "rep", None, None),
        P(("groups", "blk"), "rep", None),
    )
    out_specs = P(("groups", "blk", "rep"), None)
    return jax.shard_map(
        per_device, mesh=mesh, in_specs=in_specs, out_specs=out_specs, check_vma=False
    )
```

profile of v0, /device:TPU:0, one launch (start us, length us, event | category | flops | bytes accessed | tf_op | source)
XLA Modules:
  0.0 182.0 jit_solution(11972040666576285834)
XLA Ops:
  6.5 0.0 copy-start
  6.5 0.0 copy-start.2
  6.5 0.0 all-reduce.3.cloned.1.call-start
  6.5 0.8 convert_rsqrt_fusion
  7.3 1.2 broadcast_multiply_fusion.2
  8.6 3.1 %collective-permute-start = (f32[8,128,128]{2,1,0:T(8,128)S(1)}, f32[8,128,128]{2,1,0:T(8,128)S(1)}, u32[]{:S(2)}, u32[]{:S(2)}) collective-permute-start(f32[8,128,128]{2,1,0:T(8,128)S(1)} %bitcast.28), channel_id=1, source_target_pairs={{0,4},{4,8},{8,12},{12,0},{1,5},{5,9},{9,13},{13,1},{2,6},{6,10},{... | collective-permute-start | bytes 1572872 | tf_op jit(solution)/shard_map/ppermute | solution.py:11
  12.3 13.3 %collective-permute-done = f32[8,128,128]{2,1,0:T(8,128)S(1)} collective-permute-done((f32[8,128,128]{2,1,0:T(8,128)S(1)}, f32[8,128,128]{2,1,0:T(8,128)S(1)}, u32[]{:S(2)}, u32[]{:S(2)}) %collective-permute-start) | collective-permute-done | bytes 524320 | tf_op jit(solution)/shard_map/ppermute | solution.py:11
  25.6 0.1 broadcast_select_fusion.1
  25.6 0.8 collective-permute-start.1
  26.4 0.0 copy-done.2
  26.5 23.3 %collective-permute-done.1 = f32[8,128,128]{2,1,0:T(8,128)S(1)} collective-permute-done((f32[8,128,128]{2,1,0:T(8,128)S(1)}, f32[8,128,128]{2,1,0:T(8,128)S(1)}, u32[]{:S(2)}, u32[]{:S(2)}) %collective-permute-start.1) | collective-permute-done | bytes 524320 | tf_op jit(solution)/shard_map/ppermute | solution.py:11
  49.8 0.1 broadcast_select_fusion.3
  49.9 1.8 gather_fusion
  51.6 0.0 copy-done
  51.7 2.9 %fusion.6 = f32[24,128,128]{2,1,0:T(8,128)S(1)} fusion(f32[24,128,128]{2,1,0:T(8,128)} %gather_fusion, bf16[1,1,1,24,128,128]{5,4,3,2,1,0:T(8,128)(2,1)S(1)} %copy-done, pred[24]{0:T(512)(128)(4,1)S(1)} %compare_and_fusion), kind=kOutput, calls=%fused_computation.8 | convolution fusion | flops 604372992 | bytes 3932184 | tf_op jit(solution)/shard_map/jab,jbw->jaw/dot_general | solution.py:23
  54.5 0.0 copy-start.1
  54.6 1.6 copy.9
  56.2 0.0 copy-done.1
  56.2 2.0 %fusion.2 = f32[8,128,128]{2,0,1:T(8,128)S(1)} fusion(f32[24,128,128]{1,0,2:T(8,128)} %copy.9, s32[24]{0:T(128)S(1)} %bitcast.32, pred[24]{0:T(512)(128)(4,1)S(1)} %iota_compare_fusion.1), kind=kOutput, calls=%fused_computation.4 | convolution fusion | flops 37749120 | bytes 2097272 | tf_op jit(solution)/shard_map/jc,jaw->caw/dot_general | solution.py:35
  58.2 0.9 copy.7
  59.1 0.0 all-reduce.3.cloned.1.call-update
  59.1 0.0 all-reduce.5.cloned.1.call-start
  59.2 33.4 %all-reduce.3.cloned.1.call-done = f32[1024,128]{1,0:T(8,128)} async-done(((f32[1024,128]{1,0:T(8,128)}), f32[1024,128]{1,0:T(8,128)}) %all-reduce.3.cloned.1.call-update) | async-done | bytes 524304 | tf_op jit(solution)/shard_map/psum | solution.py:71
  92.6 1.2 broadcast_multiply_fusion.1
  93.8 1.5 collective-permute-start.2
  95.4 12.8 %collective-permute-done.2 = f32[8,128,128]{2,1,0:T(8,128)S(1)} collective-permute-done((f32[8,128,128]{2,1,0:T(8,128)S(1)}, f32[8,128,128]{2,1,0:T(8,128)S(1)}, u32[]{:S(2)}, u32[]{:S(2)}) %collective-permute-start.2) | collective-permute-done | bytes 524320 | tf_op jit(solution)/shard_map/ppermute | solution.py:11
  108.2 0.1 broadcast_select_fusion
  108.3 0.9 collective-permute-start.3
  109.2 22.5 %collective-permute-done.3 = f32[8,128,128]{2,1,0:T(8,128)S(1)} collective-permute-done((f32[8,128,128]{2,1,0:T(8,128)S(1)}, f32[8,128,128]{2,1,0:T(8,128)S(1)}, u32[]{:S(2)}, u32[]{:S(2)}) %collective-permute-start.3) | collective-permute-done | bytes 524320 | tf_op jit(solution)/shard_map/ppermute | solution.py:11
  131.6 0.1 broadcast_select_fusion.2
  131.7 1.8 gather_fusion.1
  133.5 2.9 %fusion.4 = f32[24,128,128]{2,1,0:T(8,128)S(1)} fusion(f32[24,128,128]{2,1,0:T(8,128)} %gather_fusion.1, bf16[1,1,1,24,128,128]{5,4,3,2,1,0:T(8,128)(2,1)S(1)} %copy-done, pred[24]{0:T(512)(128)(4,1)S(1)} %compare_and_fusion), kind=kOutput, calls=%fused_computation.6 | convolution fusion | flops 604372992 | bytes 3932184 | tf_op jit(solution)/shard_map/jab,jbw->jaw/dot_general | solution.py:23
  136.4 1.6 copy.10
  138.0 2.0 %fusion = f32[8,128,128]{2,0,1:T(8,128)S(1)} fusion(f32[24,128,128]{1,0,2:T(8,128)} %copy.10, s32[24]{0:T(128)S(1)} %bitcast.33, pred[24]{0:T(512)(128)(4,1)S(1)} %iota_compare_fusion.1), kind=kOutput, calls=%fused_computation.2 | convolution fusion | flops 37749120 | bytes 2097272 | tf_op jit(solution)/shard_map/jc,jaw->caw/dot_general | solution.py:35
  140.1 0.9 copy.8
  141.0 0.0 all-reduce.5.cloned.1.call-update
  141.0 0.1 dynamic-slice
  141.1 32.4 %all-reduce.5.cloned.1.call-done = f32[1024,128]{1,0:T(8,128)} async-done(((f32[1024,128]{1,0:T(8,128)}), f32[1024,128]{1,0:T(8,128)}) %all-reduce.5.cloned.1.call-update) | async-done | bytes 524304 | tf_op jit(solution)/shard_map/psum | solution.py:71
  173.5 1.7 fusion.15
  (4 shorter events, 0.0 us)
Async XLA Ops:
  6.5 45.1 %copy-start = (bf16[1,1,1,24,128,128]{5,4,3,2,1,0:T(8,128)(2,1)S(1)}, bf16[1,1,1,24,128,128]{5,4,3,2,1,0:T(8,128)(2,1)}, u32[]{:S(2)}) copy-start(bf16[1,1,1,24,128,128]{5,4,3,2,1,0:T(8,128)(2,1)} %param.10) | copy-start | bytes 2359300
  6.5 19.9 %copy-start.2 = (s32[1,1,1,24]{3,2,1,0:T(1,128)S(1)}, s32[1,1,1,24]{3,2,1,0:T(1,128)}, u32[]{:S(2)}) copy-start(s32[1,1,1,24]{3,2,1,0:T(1,128)} %param.12) | copy-start | bytes 292
  6.5 86.1 %all-reduce.3.cloned.1.call-start = ((), (), s32[]{:S(2)}) async-start(), calls=%async_computation | async-start | bytes 1048576 | tf_op jit(solution)/shard_map/psum | solution.py:71
  8.6 17.0 %collective-permute-start = (f32[8,128,128]{2,1,0:T(8,128)S(1)}, f32[8,128,128]{2,1,0:T(8,128)S(1)}, u32[]{:S(2)}, u32[]{:S(2)}) collective-permute-start(f32[8,128,128]{2,1,0:T(8,128)S(1)} %bitcast.28), channel_id=1, source_target_pairs={{0,4},{4,8},{8,12},{12,0},{1,5},{5,9},{9,13},{13,1},{2,6},{6,10},{... | collective-permute-start | bytes 1572872 | tf_op jit(solution)/shard_map/ppermute | solution.py:11
  25.6 24.1 %collective-permute-start.1 = (f32[8,128,128]{2,1,0:T(8,128)S(1)}, f32[8,128,128]{2,1,0:T(8,128)S(1)}, u32[]{:S(2)}, u32[]{:S(2)}) collective-permute-start(f32[8,128,128]{2,1,0:T(8,128)S(1)} %broadcast_select_fusion.1), channel_id=1, source_target_pairs={{0,8},{4,12},{8,0},{12,4},{1,9},{5,13},{9,1},{13,5},{2,10},{6,14},... | collective-permute-start | bytes 1572872 | tf_op jit(solution)/shard_map/ppermute | solution.py:11
  54.5 1.6 copy-start.1
  59.1 114.3 %all-reduce.5.cloned.1.call-start = ((), (), s32[]{:S(2)}) async-start(), calls=%async_computation.1 | async-start | bytes 1048576 | tf_op jit(solution)/shard_map/psum | solution.py:71
  93.8 14.4 %collective-permute-start.2 = (f32[8,128,128]{2,1,0:T(8,128)S(1)}, f32[8,128,128]{2,1,0:T(8,128)S(1)}, u32[]{:S(2)}, u32[]{:S(2)}) collective-permute-start(f32[8,128,128]{2,1,0:T(8,128)S(1)} %bitcast.26), channel_id=1, source_target_pairs={{0,4},{4,8},{8,12},{12,0},{1,5},{5,9},{9,13},{13,1},{2,6},{6,10},{... | collective-permute-start | bytes 1572872 | tf_op jit(solution)/shard_map/ppermute | solution.py:11
  108.3 23.3 %collective-permute-start.3 = (f32[8,128,128]{2,1,0:T(8,128)S(1)}, f32[8,128,128]{2,1,0:T(8,128)S(1)}, u32[]{:S(2)}, u32[]{:S(2)}) collective-permute-start(f32[8,128,128]{2,1,0:T(8,128)S(1)} %broadcast_select_fusion), channel_id=1, source_target_pairs={{0,8},{4,12},{8,0},{12,4},{1,9},{5,13},{9,1},{13,5},{2,10},{6,14},... | collective-permute-start | bytes 1572872 | tf_op jit(solution)/shard_map/ppermute | solution.py:11
Sparse Core Ops, SparseCore 0:
  59.3 33.2 all-reduce.2
  141.1 32.3 all-reduce.4
where the time goes:
time: 182 us
  waiting for transfers between devices  138 us (76%)
  between operations  14.1 us (8%)
  matrix products  9.86 us (5%)
  local copies, waits for them, and re-layouts  8.72 us (5%)
  starting transfers between devices  6.33 us (3%)
  other arithmetic  5.26 us (3%)
    ppermute x4, waiting for transfers between devices, shifted_2(): lax.ppermute(shard, axis, [(i, (i + by) % devices) for i in range(devices)])  71.9 us
    psum x2, waiting for transfers between devices, per_device(): current = lax.psum(partial_value, 'rep') * norm_scale[:, None]  65.8 us
    ppermute x4, starting transfers between devices, shifted_2(): lax.ppermute(shard, axis, [(i, (i + by) % devices) for i in range(devices)])  6.29 us
    dot_general x2, matrix products, slot_term(): jnp.einsum('jab,jbw->jaw', values, blocks, precision=lax.Precision.HIGHES...  5.78 us
    dot_general x2, matrix products, slot_term(): jnp.einsum('jc,jaw->caw', placement, products, precision=lax.Precision.HI...  4.08 us
  transfers between devices with their start and end apart: 6, of which 6 were waited for; matrix products, arithmetic and copies ran while one was open for 0% of the time, Pallas kernels for 0%

commit v1 on v0

--- a/solution.py
+++ b/solution.py
@@ -68,7 +68,12 @@
         source_panel = (current * norm_scale[:, None]).reshape(block_count, tile_size, width_count)
         partial_value = arc_product(source_panel, slots, team_index, team_count)
         partial_value = partial_value.reshape(block_count * tile_size, width_count)
-        current = lax.psum(partial_value, "rep") * norm_scale[:, None]
+
+        def answer_goods_for(raw, bus_axis="rep"):
+            v_next = lax.all_gather(raw, axis_name=bus_axis)
+            return jnp.sum(v_next, axis=0)
+
+        current = answer_goods_for(partial_value) * norm_scale[:, None]
         combined = combined + lax.dynamic_slice_in_dim(current, team_index * share_rows, share_rows)
     return combined / (LAYERS + 1.0)
 

time: 182 us -> 166 us (0.912)
  waiting for transfers between devices: 138 us -> 119 us
  other arithmetic: 5.26 us -> 7.79 us
    psum x2 -> x0, waiting for transfers between devices: 65.8 us -> none  [per_device(): current = lax.psum(partial_value, 'rep') * norm_scale[:, None]]
    all_gather x0 -> x2, waiting for transfers between devices: none -> 44.5 us  [answer_goods_for(): v_next = lax.all_gather(raw, axis_name=bus_axis)]
    reduce_sum x0 -> x2, other arithmetic: none -> 3.51 us  [answer_goods_for(): return jnp.sum(v_next, axis=0)]
    ppermute x4, waiting for transfers between devices: 71.9 us -> 74.9 us  [shifted_2(): lax.ppermute(shard, axis, [(i, (i + by) % devices) for i in range(devices)])]
where the time goes in v1:
time: 166 us
  waiting for transfers between devices  119 us (72%)
  between operations  14.1 us (8%)
  matrix products  9.86 us (6%)
  local copies, waits for them, and re-layouts  8.75 us (5%)
  other arithmetic  7.79 us (5%)
  starting transfers between devices  6.13 us (4%)
    ppermute x4, waiting for transfers between devices, shifted_2(): lax.ppermute(shard, axis, [(i, (i + by) % devices) for i in range(devices)])  74.9 us
    all_gather x2, waiting for transfers between devices, answer_goods_for(): v_next = lax.all_gather(raw, axis_name=bus_axis)  44.5 us
    ppermute x4, starting transfers between devices, shifted_2(): lax.ppermute(shard, axis, [(i, (i + by) % devices) for i in range(devices)])  6.08 us
    dot_general x2, matrix products, slot_term(): jnp.einsum('jab,jbw->jaw', values, blocks, precision=lax.Precision.HIGHES...  5.78 us
    dot_general x2, matrix products, slot_term(): jnp.einsum('jc,jaw->caw', placement, products, precision=lax.Precision.HI...  4.07 us
    gather x2, local copies, waits for them, and re-layouts, slot_term(): blocks = jnp.take(source_panel, columns, axis=0)  3.6 us
    reduce_sum x2, other arithmetic, answer_goods_for(): return jnp.sum(v_next, axis=0)  3.51 us
  transfers between devices with their start and end apart: 6, of which 6 were waited for; matrix products, arithmetic and copies ran while one was open for 0% of the time, Pallas kernels for 0%

profile of v1, /device:TPU:0, one launch (start us, length us, event | category | flops | bytes accessed | tf_op | source)
XLA Modules:
  0.0 166.1 jit_solution(12125771435981745924)
XLA Ops:
  6.5 0.0 copy-start
  6.5 0.0 copy-start.2
  6.5 0.0 all-gather.3.cloned.1.call-start
  6.5 0.8 fusion.31
  7.3 1.2 broadcast_multiply_fusion
  8.6 3.1 %collective-permute-start = (f32[8,128,128]{2,1,0:T(8,128)S(1)}, f32[8,128,128]{2,1,0:T(8,128)S(1)}, u32[]{:S(2)}, u32[]{:S(2)}) collective-permute-start(f32[8,128,128]{2,1,0:T(8,128)S(1)} %bitcast.30), channel_id=1, source_target_pairs={{0,4},{4,8},{8,12},{12,0},{1,5},{5,9},{9,13},{13,1},{2,6},{6,10},{... | collective-permute-start | bytes 1572872 | tf_op jit(solution)/shard_map/ppermute | solution.py:11
  12.3 13.3 %collective-permute-done = f32[8,128,128]{2,1,0:T(8,128)S(1)} collective-permute-done((f32[8,128,128]{2,1,0:T(8,128)S(1)}, f32[8,128,128]{2,1,0:T(8,128)S(1)}, u32[]{:S(2)}, u32[]{:S(2)}) %collective-permute-start) | collective-permute-done | bytes 524320 | tf_op jit(solution)/shard_map/ppermute | solution.py:11
  25.6 0.1 broadcast_select_fusion.1
  25.6 0.8 collective-permute-start.1
  26.4 0.0 copy-done.2
  26.5 23.3 %collective-permute-done.1 = f32[8,128,128]{2,1,0:T(8,128)S(1)} collective-permute-done((f32[8,128,128]{2,1,0:T(8,128)S(1)}, f32[8,128,128]{2,1,0:T(8,128)S(1)}, u32[]{:S(2)}, u32[]{:S(2)}) %collective-permute-start.1) | collective-permute-done | bytes 524320 | tf_op jit(solution)/shard_map/ppermute | solution.py:11
  49.8 0.1 broadcast_select_fusion.3
  49.9 1.8 %gather_fusion = f32[24,128,128]{2,1,0:T(8,128)} fusion(f32[8,128,128]{2,1,0:T(8,128)S(1)} %broadcast_select_fusion.3, s32[1024]{0:T(1024)S(1)} %pad_clamp_fusion), kind=kCustom, calls=%fused_computation.clone | custom fusion | bytes 3145824 | tf_op jit(solution)/shard_map/jit(_take)/gather | solution.py:22
  51.6 0.0 copy-done
  51.7 2.9 %fusion.4 = f32[24,128,128]{1,2,0:T(8,128)S(1)} fusion(f32[24,128,128]{2,1,0:T(8,128)} %gather_fusion, bf16[1,1,1,24,128,128]{5,4,3,2,1,0:T(8,128)(2,1)S(1)} %copy-done, pred[24]{0:T(512)(128)(4,1)S(1)} %compare_and_fusion), kind=kOutput, calls=%fused_computation.6 | convolution fusion | flops 604372992 | bytes 3932184 | tf_op jit(solution)/shard_map/jab,jbw->jaw/dot_general | solution.py:23
  54.5 0.0 copy-start.1
  54.6 1.6 copy.14
  56.2 0.0 copy-done.1
  56.2 2.0 %fusion.23 = f32[8,128,128]{2,0,1:T(8,128)S(1)} fusion(f32[24,128,128]{2,0,1:T(8,128)} %copy.14, s32[24]{0:T(128)S(1)} %bitcast.34, pred[24]{0:T(512)(128)(4,1)S(1)} %iota_compare_fusion.1), kind=kOutput, calls=%fused_computation.31 | convolution fusion | flops 37749120 | bytes 2097272 | tf_op jit(solution)/shard_map/jc,jaw->caw/dot_general | solution.py:35
  58.2 0.9 copy.15
  59.1 0.0 all-gather.3.cloned.1.call-update
  59.2 0.0 all-gather.5.cloned.1.call-start
  59.2 22.8 %all-gather.3.cloned.1.call-done = f32[4,1024,128]{2,1,0:T(8,128)} async-done(((f32[1,1024,128]{2,1,0:T(8,128)}), f32[4,1024,128]{2,1,0:T(8,128)}) %all-gather.3.cloned.1.call-update) | async-done | bytes 2097168 | tf_op jit(solution)/shard_map/all_gather | solution.py:73
  82.0 1.8 %reduce_sum.20 = f32[1024,128]{1,0:T(8,128)S(1)} reduce(f32[4,1024,128]{2,1,0:T(8,128)} %all-gather.3.cloned.1.call-done, f32[]{:T(128)} %constant.48.clone.1), dimensions={0}, to_apply=%region_0.2 | reduce | flops 393216 | bytes 2621444 | tf_op jit(solution)/shard_map/reduce_sum | solution.py:74
  83.8 0.2 multiply_multiply_fusion
  84.0 1.5 collective-permute-start.2
  85.5 14.4 %collective-permute-done.2 = f32[8,128,128]{2,1,0:T(8,128)S(1)} collective-permute-done((f32[8,128,128]{2,1,0:T(8,128)S(1)}, f32[8,128,128]{2,1,0:T(8,128)S(1)}, u32[]{:S(2)}, u32[]{:S(2)}) %collective-permute-start.2) | collective-permute-done | bytes 524320 | tf_op jit(solution)/shard_map/ppermute | solution.py:11
  99.9 0.2 broadcast_select_fusion
  100.1 0.7 collective-permute-start.3
  100.8 23.9 %collective-permute-done.3 = f32[8,128,128]{2,1,0:T(8,128)S(1)} collective-permute-done((f32[8,128,128]{2,1,0:T(8,128)S(1)}, f32[8,128,128]{2,1,0:T(8,128)S(1)}, u32[]{:S(2)}, u32[]{:S(2)}) %collective-permute-start.3) | collective-permute-done | bytes 524320 | tf_op jit(solution)/shard_map/ppermute | solution.py:11
  124.7 0.1 broadcast_select_fusion.2
  124.7 1.8 %gather_fusion.1 = f32[24,128,128]{2,1,0:T(8,128)} fusion(f32[8,128,128]{2,1,0:T(8,128)S(1)} %broadcast_select_fusion.2, s32[1024]{0:T(1024)S(1)} %pad_clamp_fusion), kind=kCustom, calls=%fused_computation.1.clone | custom fusion | bytes 3145824 | tf_op jit(solution)/shard_map/jit(_take)/gather | solution.py:22
  126.5 2.9 %fusion.7 = f32[24,128,128]{1,2,0:T(8,128)S(1)} fusion(f32[24,128,128]{2,1,0:T(8,128)} %gather_fusion.1, bf16[1,1,1,24,128,128]{5,4,3,2,1,0:T(8,128)(2,1)S(1)} %copy-done, pred[24]{0:T(512)(128)(4,1)S(1)} %compare_and_fusion), kind=kOutput, calls=%fused_computation.7 | convolution fusion | flops 604372992 | bytes 3932184 | tf_op jit(solution)/shard_map/jab,jbw->jaw/dot_general | solution.py:23
  129.4 1.6 copy.17
  131.1 2.0 %fusion.21 = f32[8,128,128]{2,0,1:T(8,128)S(1)} fusion(f32[24,128,128]{2,0,1:T(8,128)} %copy.17, s32[24]{0:T(128)S(1)} %bitcast.35, pred[24]{0:T(512)(128)(4,1)S(1)} %iota_compare_fusion.1), kind=kOutput, calls=%fused_computation.30 | convolution fusion | flops 37749120 | bytes 2097272 | tf_op jit(solution)/shard_map/jc,jaw->caw/dot_general | solution.py:35
  133.1 0.9 copy.18
  134.0 0.0 all-gather.5.cloned.1.call-update
  134.0 0.1 dynamic-slice
  134.1 21.7 %all-gather.5.cloned.1.call-done = f32[4,1024,128]{2,1,0:T(8,128)} async-done(((f32[1,1024,128]{2,1,0:T(8,128)}), f32[4,1024,128]{2,1,0:T(8,128)}) %all-gather.5.cloned.1.call-update) | async-done | bytes 2097168 | tf_op jit(solution)/shard_map/all_gather | solution.py:73
  155.8 1.8 %reduce_sum.22 = f32[1024,128]{1,0:T(8,128)S(1)} reduce(f32[4,1024,128]{2,1,0:T(8,128)} %all-gather.5.cloned.1.call-done, f32[]{:T(128)} %constant.48.clone.1), dimensions={0}, to_apply=%region_1.3 | reduce | flops 393216 | bytes 2621444 | tf_op jit(solution)/shard_map/reduce_sum | solution.py:74
  157.6 1.7 %fusion.17 = f32[256,128]{1,0:T(8,128)} fusion(f32[1024,128]{1,0:T(8,128)S(1)} %reduce_sum.22, s32[]{:T(128)S(6)} %select_n.45, f32[1024,128]{1,0:T(8,128)S(1)} %reduce_sum.20, f32[1024,128]{1,0:T(8,128)} %param.8, f32[256]{0:T(256)S(1)} %dynamic-slice), kind=kLoop, calls=%fused_computation.22 | loop fusion | flops 163840 | bytes 525316 | tf_op jit(solution)/shard_map/div | solution.py:78
  (4 shorter events, 0.0 us)
Async XLA Ops:
  6.5 45.1 %copy-start = (bf16[1,1,1,24,128,128]{5,4,3,2,1,0:T(8,128)(2,1)S(1)}, bf16[1,1,1,24,128,128]{5,4,3,2,1,0:T(8,128)(2,1)}, u32[]{:S(2)}) copy-start(bf16[1,1,1,24,128,128]{5,4,3,2,1,0:T(8,128)(2,1)} %param.10) | copy-start | bytes 2359300
  6.5 19.9 %copy-start.2 = (s32[1,1,1,24]{3,2,1,0:T(1,128)S(1)}, s32[1,1,1,24]{3,2,1,0:T(1,128)}, u32[]{:S(2)}) copy-start(s32[1,1,1,24]{3,2,1,0:T(1,128)} %param.12) | copy-start | bytes 292
  6.5 75.5 %all-gather.3.cloned.1.call-start = ((), (), s32[]{:S(2)}) async-start(), calls=%async_computation | async-start | bytes 2621440 | tf_op jit(solution)/shard_map/all_gather | solution.py:73
  8.6 17.0 %collective-permute-start = (f32[8,128,128]{2,1,0:T(8,128)S(1)}, f32[8,128,128]{2,1,0:T(8,128)S(1)}, u32[]{:S(2)}, u32[]{:S(2)}) collective-permute-start(f32[8,128,128]{2,1,0:T(8,128)S(1)} %bitcast.30), channel_id=1, source_target_pairs={{0,4},{4,8},{8,12},{12,0},{1,5},{5,9},{9,13},{13,1},{2,6},{6,10},{... | collective-permute-start | bytes 1572872 | tf_op jit(solution)/shard_map/ppermute | solution.py:11
  25.6 24.1 %collective-permute-start.1 = (f32[8,128,128]{2,1,0:T(8,128)S(1)}, f32[8,128,128]{2,1,0:T(8,128)S(1)}, u32[]{:S(2)}, u32[]{:S(2)}) collective-permute-start(f32[8,128,128]{2,1,0:T(8,128)S(1)} %broadcast_select_fusion.1), channel_id=1, source_target_pairs={{0,8},{4,12},{8,0},{12,4},{1,9},{5,13},{9,1},{13,5},{2,10},{6,14},... | collective-permute-start | bytes 1572872 | tf_op jit(solution)/shard_map/ppermute | solution.py:11
  54.5 1.6 copy-start.1
  59.2 96.7 %all-gather.5.cloned.1.call-start = ((), (), s32[]{:S(2)}) async-start(), calls=%async_computation.1 | async-start | bytes 2621440 | tf_op jit(solution)/shard_map/all_gather | solution.py:73
  84.0 15.9 %collective-permute-start.2 = (f32[8,128,128]{2,1,0:T(8,128)S(1)}, f32[8,128,128]{2,1,0:T(8,128)S(1)}, u32[]{:S(2)}, u32[]{:S(2)}) collective-permute-start(f32[8,128,128]{2,1,0:T(8,128)S(1)} %multiply_multiply_fusion), channel_id=1, source_target_pairs={{0,4},{4,8},{8,12},{12,0},{1,5},{5,9},{9,13},{13,1},{2,6},{6,10},{... | collective-permute-start | bytes 1572872 | tf_op jit(solution)/shard_map/ppermute | solution.py:11
  100.1 24.6 %collective-permute-start.3 = (f32[8,128,128]{2,1,0:T(8,128)S(1)}, f32[8,128,128]{2,1,0:T(8,128)S(1)}, u32[]{:S(2)}, u32[]{:S(2)}) collective-permute-start(f32[8,128,128]{2,1,0:T(8,128)S(1)} %broadcast_select_fusion), channel_id=1, source_target_pairs={{0,8},{4,12},{8,0},{12,4},{1,9},{5,13},{9,1},{13,5},{2,10},{6,14},... | collective-permute-start | bytes 1572872 | tf_op jit(solution)/shard_map/ppermute | solution.py:11
Sparse Core Ops, SparseCore 0:
  59.3 22.6 all-gather.2
  134.2 21.6 all-gather.4
